TPU v7x, 512 devices: a whole 4x4x16 slice. The times are simulated.
512 devices in a mesh: tm: 32 (over z, core), col: 16 (over y, x).
Axes of the slice: x: 4, y: 4, z: 16, core: 2. Of those that a mesh axis runs over, the one named last changes fastest.
Arguments:
- diag_blocks: float32 [64, 768, 768], P('tm', 'col'), may hold values from -0.5 to 2, as said below
- left_blocks: float32 [32, 768, 768], P('tm', 'col'), may hold values from -1 to 0.5
- right_blocks: float32 [32, 768, 768], P('tm', 'col'), may hold values from -1 to 0.5
Outputs:
- blocks: float32 [64, 768, 768], P('tm', 'col')
- solved: float32 [32, 2, 768, 768], P('tm', None, 'col')
Inputs may be any that keep to these rules, and one draw needn't show every extreme that they name: `diag_blocks`: every block is symmetric, and together with left_blocks, right_blocks and their transposes it forms a symmetric positive definite matrix.
All inputs are finite; a program needn't handle non-finite values.
Results may differ from a plain program's by a relative error of at most 0.00013.
Values sent between devices are 32-bit elements; how exact they have to be, the bound alone decides.
A program may use at most 64 MiB of HBM per device.

v0:
```python
import jax
import jax.numpy as jnp
from jax import lax
from jax.sharding import PartitionSpec as P


def passed_along(x, axis, by):
    peers = lax.axis_size(axis)
    return lax.ppermute(x, axis, [(i, (i + by) % peers) for i in range(peers)])


def extended(x, sides, width):
    for axis, dim in sides:
        peers, length = (lax.axis_size(axis), x.shape[dim])
        up = [(i, (i + 1) % peers) for i in range(peers)]
        down = [(j, i) for i, j in up]
        last = lax.slice_in_dim(x, length - width, length, axis=dim)
        first = lax.slice_in_dim(x, 0, width, axis=dim)
        before = lax.ppermute(last, axis, up)
        after = lax.ppermute(first, axis, down)
        x = jnp.concatenate([before, x, after], axis=dim)
    return x


def rows_dot(row_part, full_part):
    return lax.dot_general(
        row_part,
        full_part,
        (((1,), (1,)), ((), ())),
        precision=lax.Precision.HIGHEST,
        preferred_element_type=jnp.float32,
    )


def right_solve(factor, target):
    return lax.linalg.triangular_solve(
        factor, target, left_side=False, lower=True, transpose_a=True
    )


def eliminate(pivot_rows, left_rows, right_rows):
    height = pivot_rows.shape[0]
    row_start = lax.axis_index("col") * height
    pivot_full = lax.all_gather(pivot_rows, "col", axis=0, tiled=True)
    factor = jnp.linalg.cholesky(pivot_full)
    solved_left = right_solve(factor, left_rows)
    solved_right = right_solve(factor, right_rows)
    full_left, full_right = (
        lax.all_gather(solved_left, "col", axis=0, tiled=True),
        lax.all_gather(solved_right, "col", axis=0, tiled=True),
    )
    factor_rows = lax.dynamic_slice_in_dim(factor, row_start, height, 0)
    return (
        factor_rows,
        solved_left,
        solved_right,
        full_left,
        full_right,
        solved_left,
        solved_right,
    )


def shards(diag_blocks, left_blocks, right_blocks):
    even_rows = diag_blocks[0]
    odd_rows = diag_blocks[1]
    factor_one, solved_left, solved_right, full_left, full_right, back_left, back_right = eliminate(
        odd_rows, left_blocks[0], right_blocks[0]
    )
    left_gram = rows_dot(back_left, full_left)
    right_gram = rows_dot(back_right, full_right)
    upper_rows = -rows_dot(back_left, full_right)
    mirror_upper = -rows_dot(back_right, full_left)
    right_prev, mirror_lower = passed_along((right_gram, upper_rows), "tm", 1)
    reduced = even_rows - left_gram - right_prev
    factor_two, first_solved, second_solved, first_full, second_full, first_back, second_back = (
        eliminate(reduced, mirror_lower, mirror_upper)
    )
    second_grams = jnp.stack([rows_dot(first_back, first_full), rows_dot(second_back, second_full)])
    halo_rows = extended(second_grams, (("tm", 0),), 1)
    final_block = reduced - halo_rows[3] - halo_rows[0]
    blocks = jnp.stack([final_block, factor_one])
    solved = jnp.stack([solved_left, solved_right])[None]
    return (blocks, solved)


def solution(mesh):
    in_specs = (P("tm", "col", None), P("tm", "col", None), P("tm", "col", None))
    out_specs = (P("tm", "col", None), P("tm", None, "col", None))
    return jax.shard_map(shards, mesh=mesh, in_specs=in_specs, out_specs=out_specs, check_vma=False)
```

profile of v0, /device:TPU:1, one launch (start us, length us, event | category | flops | bytes accessed | tf_op | source)
XLA Modules:
  0.0 874.4 jit_solution(16462688095010835249)
XLA Ops:
  9.0 67.3 %all-gather.18.cloned.1.call-done = f32[1,768,768]{2,0,1:T(1,128)} async-done(((f32[1,48,768]{2,0,1:T(1,128)}), f32[1,768,768]{2,0,1:T(1,128)}) %all-gather.18.cloned.1.call-update) | async-done | bytes 2359312 | tf_op jit(solution)/shard_map/all_gather | solution.py:44
  86.6 11.7 %cholesky.453 = f32[128,128]{1,0:T(8,128)S(1)} custom-call(f32[128,128]{1,0:T(8,128)S(1)} %cholesky.669), custom_call_target="Cholesky" | custom-call | tf_op jit(solution)/shard_map/jit(cholesky)/cholesky | solution.py:45
  111.1 11.7 %cholesky.472 = f32[128,128]{1,0:T(8,128)S(1)} custom-call(f32[128,128]{1,0:T(8,128)S(1)} %cholesky.673), custom_call_target="Cholesky" | custom-call | tf_op jit(solution)/shard_map/jit(cholesky)/cholesky | solution.py:45
  122.8 10.0 %custom-call.44 = f32[1,128,128]{1,2,0:T(8,128)S(1)} custom-call(f32[1,128,128]{2,1,0:T(8,128)S(1)} %get-tuple-element.86), custom_call_target="InvertDiagBlocksLowerTriangular" | custom-call | tf_op jit(solution)/shard_map/jit(cholesky)/cholesky | solution.py:45
  134.7 11.7 %cholesky.493 = f32[128,128]{1,0:T(8,128)S(1)} custom-call(f32[128,128]{1,0:T(8,128)S(1)} %cholesky.678), custom_call_target="Cholesky" | custom-call | tf_op jit(solution)/shard_map/jit(cholesky)/cholesky | solution.py:45
  158.8 12.1 %cholesky.512 = f32[128,128]{1,0:T(8,128)S(1)} custom-call(f32[128,128]{1,0:T(8,128)S(1)} %cholesky.683), custom_call_target="Cholesky" | custom-call | tf_op jit(solution)/shard_map/jit(cholesky)/cholesky | solution.py:45
  183.2 11.7 %cholesky.531 = f32[128,128]{1,0:T(8,128)S(1)} custom-call(f32[128,128]{1,0:T(8,128)S(1)} %cholesky.688), custom_call_target="Cholesky" | custom-call | tf_op jit(solution)/shard_map/jit(cholesky)/cholesky | solution.py:45
  207.0 11.9 %cholesky.548 = f32[128,128]{1,0:T(8,128)S(1)} custom-call(f32[128,128]{1,0:T(8,128)S(1)} %convolution_subtract_fusion.5), custom_call_target="Cholesky" | custom-call | tf_op jit(solution)/shard_map/jit(cholesky)/cholesky | solution.py:45
  226.6 17.4 %while.8 = (s32[]{:T(128)}, f32[768,768]{1,0:T(8,128)}, s32[6,2]{0,1:T(2,128)S(1)}, f32[6,128,128]{2,1,0:T(8,128)S(1)}, s32[]{:T(128)}) while((s32[]{:T(128)}, f32[768,768]{1,0:T(8,128)}, s32[6,2]{0,1:T(2,128)S(1)}, f32[6,128,128]{2,1,0:T(8,128)S(1)}, s32[]{:T(128)}) %tuple.107), condition=%wide.while_cond, body=%wide.while_body.sunk | while | flops 2 | bytes 131189 | solution.py:36
  243.9 59.0 %custom-call.48 = f32[6,128,128]{1,2,0:T(8,128)S(1)} custom-call(f32[6,128,128]{2,1,0:T(8,128)S(1)} %get-tuple-element.30), custom_call_target="InvertDiagBlocksLowerTriangular" | custom-call | tf_op jit(solution)/shard_map/triangular_solve/custom-call.5 | solution.py:36
  319.3 52.2 %all-gather.10.cloned.1.call-done = f32[768,768]{1,0:T(8,128)} async-done(((f32[48,768]{1,0:T(8,128)}), f32[768,768]{1,0:T(8,128)}) %all-gather.10.cloned.1.call-update) | async-done | bytes 2359312 | tf_op jit(solution)/shard_map/all_gather | solution.py:50
  378.6 56.7 %all-gather.8.cloned.1.call-done = f32[768,768]{1,0:T(8,128)} async-done(((f32[48,768]{1,0:T(8,128)}), f32[768,768]{1,0:T(8,128)}) %all-gather.8.cloned.1.call-update) | async-done | bytes 2359312 | tf_op jit(solution)/shard_map/all_gather | solution.py:49
  442.4 58.0 %all-gather.12.cloned.1.call-done = f32[768,768]{1,0:T(8,128)} async-done(((f32[48,768]{1,0:T(8,128)}), f32[768,768]{1,0:T(8,128)}) %all-gather.12.cloned.1.call-update) | async-done | bytes 2359312 | tf_op jit(solution)/shard_map/all_gather | solution.py:44
  507.5 11.7 %cholesky.563 = f32[128,128]{1,0:T(8,128)S(1)} custom-call(f32[128,128]{1,0:T(8,128)S(1)} %cholesky.692), custom_call_target="Cholesky" | custom-call | tf_op jit(solution)/shard_map/jit(cholesky)/cholesky | solution.py:45
  532.7 11.7 %cholesky.582 = f32[128,128]{1,0:T(8,128)S(1)} custom-call(f32[128,128]{1,0:T(8,128)S(1)} %cholesky.696), custom_call_target="Cholesky" | custom-call | tf_op jit(solution)/shard_map/jit(cholesky)/cholesky | solution.py:45
  545.1 9.9 %custom-call.51 = f32[1,128,128]{1,2,0:T(8,128)S(1)} custom-call(f32[1,128,128]{2,1,0:T(8,128)S(1)} %get-tuple-element.70), custom_call_target="InvertDiagBlocksLowerTriangular" | custom-call | tf_op jit(solution)/shard_map/jit(cholesky)/cholesky | solution.py:45
  557.0 11.7 %cholesky.603 = f32[128,128]{1,0:T(8,128)S(1)} custom-call(f32[128,128]{1,0:T(8,128)S(1)} %cholesky.701), custom_call_target="Cholesky" | custom-call | tf_op jit(solution)/shard_map/jit(cholesky)/cholesky | solution.py:45
  581.1 11.9 %cholesky.622 = f32[128,128]{1,0:T(8,128)S(1)} custom-call(f32[128,128]{1,0:T(8,128)S(1)} %cholesky.706), custom_call_target="Cholesky" | custom-call | tf_op jit(solution)/shard_map/jit(cholesky)/cholesky | solution.py:45
  605.4 11.7 %cholesky.641 = f32[128,128]{1,0:T(8,128)S(1)} custom-call(f32[128,128]{1,0:T(8,128)S(1)} %cholesky.711), custom_call_target="Cholesky" | custom-call | tf_op jit(solution)/shard_map/jit(cholesky)/cholesky | solution.py:45
  629.1 12.1 %cholesky.658 = f32[128,128]{1,0:T(8,128)S(1)} custom-call(f32[128,128]{1,0:T(8,128)S(1)} %slice_subtract_fusion.4), custom_call_target="Cholesky" | custom-call | tf_op jit(solution)/shard_map/jit(cholesky)/cholesky | solution.py:45
  647.2 17.3 %while.9 = (s32[]{:T(128)}, f32[768,768]{1,0:T(8,128)}, s32[6,2]{0,1:T(2,128)S(1)}, f32[6,128,128]{2,1,0:T(8,128)S(1)}, s32[]{:T(128)}) while((s32[]{:T(128)}, f32[768,768]{1,0:T(8,128)}, s32[6,2]{0,1:T(2,128)S(1)}, f32[6,128,128]{2,1,0:T(8,128)S(1)}, s32[]{:T(128)}) %tuple.125), condition=%wide.while_cond.clone.1, body=%wide.while_body.clone.1.sunk | while | flops 2 | bytes 131189 | solution.py:36
  665.2 59.8 %custom-call.55 = f32[6,128,128]{1,2,0:T(8,128)S(1)} custom-call(f32[6,128,128]{2,1,0:T(8,128)} %copy-done.15), custom_call_target="InvertDiagBlocksLowerTriangular" | custom-call | tf_op jit(solution)/shard_map/triangular_solve/custom-call.5 | solution.py:36
  749.1 44.4 %all-gather.16.cloned.1.call-done = f32[768,768]{1,0:T(8,128)} async-done(((f32[48,768]{1,0:T(8,128)}), f32[768,768]{1,0:T(8,128)}) %all-gather.16.cloned.1.call-update) | async-done | bytes 2359312 | tf_op jit(solution)/shard_map/all_gather | solution.py:50
  800.6 55.9 %all-gather.14.cloned.1.call-done = f32[768,768]{1,0:T(8,128)} async-done(((f32[48,768]{1,0:T(8,128)}), f32[768,768]{1,0:T(8,128)}) %all-gather.14.cloned.1.call-update) | async-done | bytes 2359312 | tf_op jit(solution)/shard_map/all_gather | solution.py:49
  (223 shorter events, 236.7 us)
Async XLA Ops:
  7.2 69.1 %all-gather.18.cloned.1.call-start = ((), (), s32[]{:S(2)}) async-start(), calls=%async_computation.5 | async-start | bytes 2506752 | tf_op jit(solution)/shard_map/all_gather | solution.py:44
  9.0 362.5 %all-gather.10.cloned.1.call-start = ((), (), s32[]{:S(2)}) async-start(), calls=%async_computation.1 | async-start | bytes 2506752 | tf_op jit(solution)/shard_map/all_gather | solution.py:50
  76.3 6.9 copy-start
  85.1 1.4 copy-start.5
  224.1 78.9 %copy-start.17 = (f32[1,48,768]{2,1,0:T(8,128)S(1)}, f32[1,48,768]{2,1,0:T(8,128)}, u32[]{:S(2)}) copy-start(f32[1,48,768]{2,1,0:T(8,128)} %param.8) | copy-start | bytes 442372
  226.5 84.6 %copy-start.18 = (f32[1,48,768]{2,1,0:T(8,128)S(1)}, f32[1,48,768]{2,1,0:T(8,128)}, u32[]{:S(2)}) copy-start(f32[1,48,768]{2,1,0:T(8,128)} %param.7) | copy-start | bytes 442372
  311.0 60.4 %copy-start.9 = (f32[48,768]{1,0:T(8,128)S(1)}, f32[48,768]{1,0:T(8,128)}, u32[]{:S(2)}) copy-start(f32[48,768]{1,0:T(8,128)} %copy-done.8) | copy-start | bytes 442372
  311.0 124.2 %all-gather.8.cloned.1.call-start = ((), (), s32[]{:S(2)}) async-start(), calls=%async_computation | async-start | bytes 2506752 | tf_op jit(solution)/shard_map/all_gather | solution.py:49
  313.7 121.6 %copy-start.16 = (f32[2,48,768]{2,1,0:T(8,128)S(1)}, f32[2,48,768]{2,1,0:T(8,128)}, u32[]{:S(2)}) copy-start(f32[2,48,768]{2,1,0:T(8,128)} %param.6) | copy-start | bytes 884740
  319.2 116.1 %copy-start.7 = (f32[48,768]{1,0:T(8,128)S(1)}, f32[48,768]{1,0:T(8,128)}, u32[]{:S(2)}) copy-start(f32[48,768]{1,0:T(8,128)} %copy-done.6) | copy-start | bytes 442372
  319.2 181.2 %all-gather.12.cloned.1.call-start = ((), (), s32[]{:S(2)}) async-start(), calls=%async_computation.2 | async-start | bytes 2506752 | tf_op jit(solution)/shard_map/all_gather | solution.py:44
  375.4 59.9 %collective-permute-start = (f32[48,768]{1,0:T(8,128)S(1)}, f32[48,768]{1,0:T(8,128)S(1)}, u32[]{:S(2)}, u32[]{:S(2)}) collective-permute-start(f32[48,768]{1,0:T(8,128)S(1)} %fusion.179), channel_id=1, source_target_pairs={{0,16},{16,32},{32,48},{48,64},{64,80},{80,96},{96,112},{112,128},... | collective-permute-start | bytes 442376 | tf_op jit(solution)/shard_map/ppermute | solution.py:9
  435.3 4.8 copy-start.3
  440.1 353.4 %all-gather.16.cloned.1.call-start = ((), (), s32[]{:S(2)}) async-start(), calls=%async_computation.4 | async-start | bytes 2506752 | tf_op jit(solution)/shard_map/all_gather | solution.py:50
  500.4 3.7 copy-start.1
  506.1 1.4 copy-start.4
  647.2 86.2 %copy-start.2 = (f32[768,768]{1,0:T(8,128)S(1)}, f32[768,768]{1,0:T(8,128)}, u32[]{:S(2)}) copy-start(f32[768,768]{1,0:T(8,128)} %all-gather.10.cloned.1.call-done) | copy-start | bytes 7077892
  733.1 60.4 %copy-start.12 = (f32[48,768]{1,0:T(8,128)S(1)}, f32[48,768]{1,0:T(8,128)}, u32[]{:S(2)}) copy-start(f32[48,768]{1,0:T(8,128)} %copy-done.11) | copy-start | bytes 442372
  733.1 123.5 %all-gather.14.cloned.1.call-start = ((), (), s32[]{:S(2)}) async-start(), calls=%async_computation.3 | async-start | bytes 2506752 | tf_op jit(solution)/shard_map/all_gather | solution.py:49
  735.6 5.3 collective-permute-start.1
  749.0 107.5 %copy-start.14 = (f32[48,768]{1,0:T(8,128)S(1)}, f32[48,768]{1,0:T(8,128)}, u32[]{:S(2)}) copy-start(f32[48,768]{1,0:T(8,128)} %copy-done.13) | copy-start | bytes 442372
  797.4 69.2 %copy-start.10 = (f32[48,768]{1,0:T(8,128)S(1)}, f32[48,768]{1,0:T(8,128)}, u32[]{:S(2)}) copy-start(f32[48,768]{1,0:T(8,128)} %fusion.4) | copy-start | bytes 442372
  797.4 66.8 %collective-permute-start.3 = (f32[1,48,768]{2,1,0:T(8,128)S(1)}, f32[1,48,768]{2,1,0:T(8,128)S(1)}, u32[]{:S(2)}, u32[]{:S(2)}) collective-permute-start(f32[1,48,768]{2,1,0:T(8,128)S(1)} %convolution_bitcast_fusion), channel_id=1, source_target_pairs={{0,16},{16,32},{32,48},{48,64},{64,80},{80,96},{96,112},{112,128},... | collective-permute-start | bytes 442376 | tf_op jit(solution)/shard_map/ppermute | solution.py:19
  860.5 6.1 collective-permute-start.2
  (5 other events, 3.4 us)
Sparse Core Ops, SparseCore 0:
  11.6 64.6 all-gather.17
  311.1 60.2 all-gather.9
  375.0 60.1 all-gather.7
  440.2 60.1 all-gather.11
  733.2 60.2 all-gather.15
  796.3 60.1 all-gather.13
where the time goes:
time: 885 us; the launch traced here: 874 us
  other arithmetic  376 us (42%)
  waiting for transfers between devices  339 us (38%)
  matrix products  70.1 us (8%)
  local copies, waits for them, and re-layouts  54.3 us (6%)
  between operations  22.7 us (3%)
  starting transfers between devices  12.2 us (1%)
    another operation x45, other arithmetic, eliminate(): factor = jnp.linalg.cholesky(pivot_full)  248 us
    all_gather x2, waiting for transfers between devices, eliminate(): pivot_full = lax.all_gather(pivot_rows, 'col', axis=0, tiled=True)  125 us
    another operation x5, other arithmetic, right_solve(): lax.linalg.triangular_solve(factor, target, left_side=False, lower=True,...  123 us
    all_gather x2, waiting for transfers between devices, eliminate(): lax.all_gather(solved_left, 'col', axis=0, tiled=True)  113 us
    all_gather x2, waiting for transfers between devices, eliminate(): lax.all_gather(solved_right, 'col', axis=0, tiled=True)  96.6 us
    another operation x39, local copies, waits for them, and re-layouts, right_solve(): lax.linalg.triangular_solve(factor, target, left_side=False, lower=True,...  34.5 us
    another operation x44, matrix products, right_solve(): lax.linalg.triangular_solve(factor, target, left_side=False, lower=True,...  29.3 us
    dot_general x6, matrix products, rows_dot(): lax.dot_general(row_part, full_part, (((1,), (1,)), ((), ())), precision=...  21.1 us
  transfers between devices with their start and end apart: 10, of which 8 were waited for; matrix products, arithmetic and copies ran while one was open for 4% of the time, Pallas kernels for 0%

commit v1 on v0

--- a/solution.py
+++ b/solution.py
@@ -46,7 +46,9 @@
     solved_left = right_solve(factor, left_rows)
     solved_right = right_solve(factor, right_rows)
     full_left, full_right = (
-        lax.all_gather(solved_left, "col", axis=0, tiled=True),
+        jnp.concatenate(
+            lax.all_to_all(jnp.stack([solved_left] * lax.axis_size("col")), "col", 0, 0), axis=0
+        ),
         lax.all_gather(solved_right, "col", axis=0, tiled=True),
     )
     factor_rows = lax.dynamic_slice_in_dim(factor, row_start, height, 0)

time: 885 us -> 807 us (0.912)
  waiting for transfers between devices: 339 us -> 240 us
  starting transfers between devices: 12.2 us -> 23.6 us
  other arithmetic: 376 us -> 386 us
    all_gather x2 -> x0, waiting for transfers between devices: 113 us -> none  [eliminate(): lax.all_gather(solved_left, 'col', axis=0, tiled=True)]
    all_to_all x0 -> x2, waiting for transfers between devices: none -> 30.7 us  [eliminate(): lax.all_to_all(jnp.stack([solved_left] * lax.axis_size('col')), 'col', 0, 0)]
    all_gather x2, waiting for transfers between devices: 96.6 us -> 85.3 us  [eliminate(): lax.all_gather(solved_right, 'col', axis=0, tiled=True)]
    another operation x45, other arithmetic: 248 us -> 258 us  [eliminate(): factor = jnp.linalg.cholesky(pivot_full)]
  transfers between devices with their start and end apart: 10 -> 10, of which waited for: 8 -> 7; matrix products, arithmetic and copies ran while one was open for 4% -> 33% of each run, Pallas kernels for 0% -> 0%
where the time goes in v1:
time: 807 us; the launch traced here: 795 us
  other arithmetic  386 us (48%)
  waiting for transfers between devices  240 us (30%)
  matrix products  66.6 us (8%)
  local copies, waits for them, and re-layouts  56.6 us (7%)
  starting transfers between devices  23.6 us (3%)
  between operations  22.6 us (3%)
    another operation x45, other arithmetic, eliminate(): factor = jnp.linalg.cholesky(pivot_full)  258 us
    another operation x5, other arithmetic, right_solve(): lax.linalg.triangular_solve(factor, target, left_side=False, lower=True,...  122 us
    all_gather x2, waiting for transfers between devices, eliminate(): pivot_full = lax.all_gather(pivot_rows, 'col', axis=0, tiled=True)  121 us
    all_gather x2, waiting for transfers between devices, eliminate(): lax.all_gather(solved_right, 'col', axis=0, tiled=True)  85.3 us
    another operation x39, local copies, waits for them, and re-layouts, right_solve(): lax.linalg.triangular_solve(factor, target, left_side=False, lower=True,...  35.1 us
    all_to_all x2, waiting for transfers between devices, eliminate(): lax.all_to_all(jnp.stack([solved_left] * lax.axis_size('col')), 'col', 0, 0)  30.7 us
    another operation x44, matrix products, right_solve(): lax.linalg.triangular_solve(factor, target, left_side=False, lower=True,...  29.3 us
    another operation x20, matrix products, eliminate(): factor = jnp.linalg.cholesky(pivot_full)  19.6 us
  transfers between devices with their start and end apart: 10, of which 7 were waited for; matrix products, arithmetic and copies ran while one was open for 33% of the time, Pallas kernels for 0%

profile of v1, /device:TPU:1, one launch (start us, length us, event | category | flops | bytes accessed | tf_op | source)
XLA Modules:
  0.0 795.0 jit_solution(2484614803483796823)
XLA Ops:
  9.0 67.3 %all-gather.12.cloned.1.call-done = f32[1,768,768]{2,0,1:T(1,128)} async-done(((f32[1,48,768]{2,0,1:T(1,128)}), f32[1,768,768]{2,0,1:T(1,128)}) %all-gather.12.cloned.1.call-update) | async-done | bytes 2359312 | tf_op jit(solution)/shard_map/all_gather | solution.py:44
  86.5 11.7 %cholesky.453 = f32[128,128]{1,0:T(8,128)S(1)} custom-call(f32[128,128]{1,0:T(8,128)S(1)} %cholesky.669), custom_call_target="Cholesky" | custom-call | tf_op jit(solution)/shard_map/jit(cholesky)/cholesky | solution.py:45
  98.3 9.8 %custom-call.43 = f32[1,128,128]{1,2,0:T(8,128)S(1)} custom-call(f32[1,128,128]{2,1,0:T(8,128)S(1)} %get-tuple-element.89), custom_call_target="InvertDiagBlocksLowerTriangular" | custom-call | tf_op jit(solution)/shard_map/jit(cholesky)/cholesky | solution.py:45
  111.1 11.7 %cholesky.472 = f32[128,128]{1,0:T(8,128)S(1)} custom-call(f32[128,128]{1,0:T(8,128)S(1)} %cholesky.673), custom_call_target="Cholesky" | custom-call | tf_op jit(solution)/shard_map/jit(cholesky)/cholesky | solution.py:45
  122.8 18.6 %custom-call.44 = f32[1,128,128]{1,2,0:T(8,128)S(1)} custom-call(f32[1,128,128]{2,1,0:T(8,128)S(1)} %get-tuple-element.86), custom_call_target="InvertDiagBlocksLowerTriangular" | custom-call | tf_op jit(solution)/shard_map/jit(cholesky)/cholesky | solution.py:45
  143.3 11.7 %cholesky.493 = f32[128,128]{1,0:T(8,128)S(1)} custom-call(f32[128,128]{1,0:T(8,128)S(1)} %cholesky.678), custom_call_target="Cholesky" | custom-call | tf_op jit(solution)/shard_map/jit(cholesky)/cholesky | solution.py:45
  167.5 12.1 %cholesky.512 = f32[128,128]{1,0:T(8,128)S(1)} custom-call(f32[128,128]{1,0:T(8,128)S(1)} %cholesky.683), custom_call_target="Cholesky" | custom-call | tf_op jit(solution)/shard_map/jit(cholesky)/cholesky | solution.py:45
  191.8 11.7 %cholesky.531 = f32[128,128]{1,0:T(8,128)S(1)} custom-call(f32[128,128]{1,0:T(8,128)S(1)} %cholesky.688), custom_call_target="Cholesky" | custom-call | tf_op jit(solution)/shard_map/jit(cholesky)/cholesky | solution.py:45
  215.6 11.9 %cholesky.548 = f32[128,128]{1,0:T(8,128)S(1)} custom-call(f32[128,128]{1,0:T(8,128)S(1)} %convolution_subtract_fusion.5), custom_call_target="Cholesky" | custom-call | tf_op jit(solution)/shard_map/jit(cholesky)/cholesky | solution.py:45
  235.1 17.4 %while.8 = (s32[]{:T(128)}, f32[768,768]{1,0:T(8,128)}, s32[6,2]{0,1:T(2,128)S(1)}, f32[6,128,128]{2,1,0:T(8,128)S(1)}, s32[]{:T(128)}) while((s32[]{:T(128)}, f32[768,768]{1,0:T(8,128)}, s32[6,2]{0,1:T(2,128)S(1)}, f32[6,128,128]{2,1,0:T(8,128)S(1)}, s32[]{:T(128)}) %tuple.107), condition=%wide.while_cond, body=%wide.while_body.sunk | while | flops 2 | bytes 131189 | solution.py:36
  252.5 59.0 %custom-call.48 = f32[6,128,128]{1,2,0:T(8,128)S(1)} custom-call(f32[6,128,128]{2,1,0:T(8,128)S(1)} %get-tuple-element.30), custom_call_target="InvertDiagBlocksLowerTriangular" | custom-call | tf_op jit(solution)/shard_map/triangular_solve/custom-call.5 | solution.py:36
  332.9 62.2 %all-gather.6.cloned.1.call-done = f32[768,768]{1,0:T(8,128)} async-done(((f32[48,768]{1,0:T(8,128)}), f32[768,768]{1,0:T(8,128)}) %all-gather.6.cloned.1.call-update) | async-done | bytes 2359312 | tf_op jit(solution)/shard_map/all_gather | solution.py:52
  414.5 53.7 %all-gather.8.cloned.1.call-done = f32[768,768]{1,0:T(8,128)} async-done(((f32[48,768]{1,0:T(8,128)}), f32[768,768]{1,0:T(8,128)}) %all-gather.8.cloned.1.call-update) | async-done | bytes 2359312 | tf_op jit(solution)/shard_map/all_gather | solution.py:44
  475.2 11.7 %cholesky.563 = f32[128,128]{1,0:T(8,128)S(1)} custom-call(f32[128,128]{1,0:T(8,128)S(1)} %cholesky.692), custom_call_target="Cholesky" | custom-call | tf_op jit(solution)/shard_map/jit(cholesky)/cholesky | solution.py:45
  501.0 12.5 %cholesky.582 = f32[128,128]{1,0:T(8,128)S(1)} custom-call(f32[128,128]{1,0:T(8,128)} %cholesky.696), custom_call_target="Cholesky" | custom-call | tf_op jit(solution)/shard_map/jit(cholesky)/cholesky | solution.py:45
  514.9 10.8 %custom-call.51 = f32[1,128,128]{1,2,0:T(8,128)S(1)} custom-call(f32[1,128,128]{2,1,0:T(8,128)} %get-tuple-element.70), custom_call_target="InvertDiagBlocksLowerTriangular" | custom-call | tf_op jit(solution)/shard_map/jit(cholesky)/cholesky | solution.py:45
  527.6 11.7 %cholesky.603 = f32[128,128]{1,0:T(8,128)S(1)} custom-call(f32[128,128]{1,0:T(8,128)S(1)} %cholesky.701), custom_call_target="Cholesky" | custom-call | tf_op jit(solution)/shard_map/jit(cholesky)/cholesky | solution.py:45
  551.7 11.9 %cholesky.622 = f32[128,128]{1,0:T(8,128)S(1)} custom-call(f32[128,128]{1,0:T(8,128)S(1)} %cholesky.706), custom_call_target="Cholesky" | custom-call | tf_op jit(solution)/shard_map/jit(cholesky)/cholesky | solution.py:45
  575.9 11.7 %cholesky.641 = f32[128,128]{1,0:T(8,128)S(1)} custom-call(f32[128,128]{1,0:T(8,128)S(1)} %cholesky.711), custom_call_target="Cholesky" | custom-call | tf_op jit(solution)/shard_map/jit(cholesky)/cholesky | solution.py:45
  599.6 12.0 %cholesky.658 = f32[128,128]{1,0:T(8,128)S(1)} custom-call(f32[128,128]{1,0:T(8,128)S(1)} %slice_subtract_fusion.4), custom_call_target="Cholesky" | custom-call | tf_op jit(solution)/shard_map/jit(cholesky)/cholesky | solution.py:45
  617.7 17.9 %while.9 = (s32[]{:T(128)}, f32[768,768]{1,0:T(8,128)}, s32[6,2]{0,1:T(2,128)S(1)}, f32[6,128,128]{2,1,0:T(8,128)S(1)}, s32[]{:T(128)}) while((s32[]{:T(128)}, f32[768,768]{1,0:T(8,128)}, s32[6,2]{0,1:T(2,128)S(1)}, f32[6,128,128]{2,1,0:T(8,128)S(1)}, s32[]{:T(128)}) %tuple.121), condition=%wide.while_cond.clone.1, body=%wide.while_body.clone.1.sunk | while | flops 2 | bytes 131189 | solution.py:36
  635.5 59.0 %custom-call.55 = f32[6,128,128]{1,2,0:T(8,128)S(1)} custom-call(f32[6,128,128]{2,1,0:T(8,128)S(1)} %get-tuple-element.32), custom_call_target="InvertDiagBlocksLowerTriangular" | custom-call | tf_op jit(solution)/shard_map/triangular_solve/custom-call.5 | solution.py:36
  715.7 30.7 %all-to-all-done.1 = f32[16,48,768]{2,1,0:T(8,128)S(1)} async-done(((f32[16,48,768]{2,1,0:T(8,128)}), f32[16,48,768]{2,1,0:T(8,128)S(1)}, u32[]{:S(2)}, u32[]{:S(2)}) %all-to-all-start.1) | async-done | bytes 2359328 | tf_op jit(solution)/shard_map/all_to_all | solution.py:50
  754.9 23.1 %all-gather.10.cloned.1.call-done = f32[768,768]{1,0:T(8,128)} async-done(((f32[48,768]{1,0:T(8,128)}), f32[768,768]{1,0:T(8,128)}) %all-gather.10.cloned.1.call-update) | async-done | bytes 2359312 | tf_op jit(solution)/shard_map/all_gather | solution.py:52
  (211 shorter events, 235.8 us)
Async XLA Ops:
  7.2 69.1 %all-gather.12.cloned.1.call-start = ((), (), s32[]{:S(2)}) async-start(), calls=%async_computation.5 | async-start | bytes 2506752 | tf_op jit(solution)/shard_map/all_gather | solution.py:44
  9.0 386.1 %all-gather.6.cloned.1.call-start = ((), (), s32[]{:S(2)}) async-start(), calls=%async_computation.2 | async-start | bytes 2506752 | tf_op jit(solution)/shard_map/all_gather | solution.py:52
  76.3 6.8 copy-start.1
  85.1 1.4 copy-start.4
  232.6 78.8 %copy-start.11 = (f32[1,48,768]{2,1,0:T(8,128)S(1)}, f32[1,48,768]{2,1,0:T(8,128)}, u32[]{:S(2)}) copy-start(f32[1,48,768]{2,1,0:T(8,128)} %param.8) | copy-start | bytes 442372
  235.0 84.5 %copy-start.12 = (f32[1,48,768]{2,1,0:T(8,128)S(1)}, f32[1,48,768]{2,1,0:T(8,128)}, u32[]{:S(2)}) copy-start(f32[1,48,768]{2,1,0:T(8,128)} %param.7) | copy-start | bytes 442372
  318.9 0.7 copy-start.5
  328.6 66.5 %copy-start.6 = (f32[48,768]{1,0:T(8,128)S(1)}, f32[48,768]{1,0:T(8,128)}, u32[]{:S(2)}) copy-start(f32[48,768]{1,0:T(8,128)} %copy-done.5) | copy-start | bytes 442372
  328.6 73.7 %all-to-all-start = ((f32[16,48,768]{2,1,0:T(8,128)}), f32[16,48,768]{2,1,0:T(8,128)S(1)}, u32[]{:S(2)}, u32[]{:S(2)}) async-start(f32[16,48,768]{2,1,0:T(8,128)} %stack.20), calls=%async_computation | async-start | bytes 4718592 | tf_op jit(solution)/shard_map/all_to_all | solution.py:50
  332.8 71.5 %copy-start.10 = (f32[2,48,768]{2,1,0:T(8,128)S(1)}, f32[2,48,768]{2,1,0:T(8,128)}, u32[]{:S(2)}) copy-start(f32[2,48,768]{2,1,0:T(8,128)} %param.6) | copy-start | bytes 884740
  332.8 135.3 %all-gather.8.cloned.1.call-start = ((), (), s32[]{:S(2)}) async-start(), calls=%async_computation.3 | async-start | bytes 2506752 | tf_op jit(solution)/shard_map/all_gather | solution.py:44
  399.0 5.3 collective-permute-start
  407.4 370.7 %all-gather.10.cloned.1.call-start = ((), (), s32[]{:S(2)}) async-start(), calls=%async_computation.4 | async-start | bytes 2506752 | tf_op jit(solution)/shard_map/all_gather | solution.py:52
  407.4 2.3 copy-start.2
  412.0 290.6 %collective-permute-start.1 = (f32[48,768]{1,0:T(8,128)S(1)}, f32[48,768]{1,0:T(8,128)S(1)}, u32[]{:S(2)}, u32[]{:S(2)}) collective-permute-start(f32[48,768]{1,0:T(8,128)S(1)} %convolution_negate_fusion.1), channel_id=1, source_target_pairs={{0,16},{16,32},{32,48},{48,64},{64,80},{80,96},{96,112},{112,128},... | collective-permute-start | bytes 442376 | tf_op jit(solution)/shard_map/ppermute | solution.py:9
  468.2 3.6 copy-start
  473.8 1.4 copy-start.3
  701.9 0.7 copy-start.8
  711.6 34.8 %all-to-all-start.1 = ((f32[16,48,768]{2,1,0:T(8,128)}), f32[16,48,768]{2,1,0:T(8,128)S(1)}, u32[]{:S(2)}, u32[]{:S(2)}) async-start(f32[16,48,768]{2,1,0:T(8,128)} %stack.21), calls=%async_computation.1 | async-start | bytes 4718592 | tf_op jit(solution)/shard_map/all_to_all | solution.py:50
  715.7 62.3 %copy-start.9 = (f32[48,768]{1,0:T(8,128)S(1)}, f32[48,768]{1,0:T(8,128)}, u32[]{:S(2)}) copy-start(f32[48,768]{1,0:T(8,128)} %copy-done.8) | copy-start | bytes 442372
  748.7 38.6 %copy-start.7 = (f32[48,768]{1,0:T(8,128)S(1)}, f32[48,768]{1,0:T(8,128)}, u32[]{:S(2)}) copy-start(f32[48,768]{1,0:T(8,128)} %fusion.4) | copy-start | bytes 442372
  748.8 38.1 %collective-permute-start.2 = (f32[1,48,768]{2,1,0:T(8,128)S(1)}, f32[1,48,768]{2,1,0:T(8,128)S(1)}, u32[]{:S(2)}, u32[]{:S(2)}) collective-permute-start(f32[1,48,768]{2,1,0:T(8,128)S(1)} %convolution_bitcast_fusion.1), channel_id=1, source_target_pairs={{16,0},{32,16},{48,32},{64,48},{80,64},{96,80},{112,96},{128,112},... | collective-permute-start | bytes 442376 | tf_op jit(solution)/shard_map/ppermute | solution.py:20
  782.0 5.3 collective-permute-start.3
Sparse Core Ops, SparseCore 0:
  11.6 64.6 all-gather.11
  319.7 75.3 all-gather.5
  407.5 60.6 all-gather.7
  702.7 75.2 all-gather.9
